TPU v7x, 32 devices: a whole 2x2x4 slice. The times are simulated.
32 devices in a mesh: rows: 8 (over z, y), cols: 4 (over x, core).
Axes of the slice: x: 2, y: 2, z: 4, core: 2. Of those that a mesh axis runs over, the one named last changes fastest.
Arguments:
- feats_t: bfloat16 [128, 16384], P('cols', 'rows'), may hold values from -6 to 6
- adj_index: int32 [128, 16], replicated, may hold values from 0 to 127, as said below
- adj_weight: bfloat16 [128, 16, 128, 128], P('rows'), as said below
- weight: bfloat16 [128, 256], replicated, may hold values from -0.5 to 0.5
- cotangent_t: bfloat16 [256, 16384], P('cols', 'rows'), may hold values from -6 to 6
Outputs:
- output_t: bfloat16 [256, 16384], P('cols', 'rows')
- weight_grad: float32 [128, 256], P('cols')
- feat_grad: float32 [128, 16384], P('cols', 'rows')
Inputs may be any that keep to these rules, and one draw needn't show every extreme that they name: `adj_index`: slot 0 of row block i names block i itself. Blocks are grouped 16 to a device in order. Slot 1 names a block of the next device (device index plus one, cyclically). The row blocks of one device name at most 4 distinct blocks of any other device, and exactly 4 of the next one. A block may stand in several slots of one row block. `adj_weight`: Nonnegative; about one entry in eight is nonzero.
All inputs are finite; a program needn't handle non-finite values.
Results may differ from a plain program's by a relative error of at most 0.0054.
Values may be sent and summed in bfloat16 or wider, within the bound.
No kernel may reach another device: no remote copies, remote signals or barrier semaphores. Data moves between devices by JAX's collectives and lax.ppermute only.
A program may use at most 128 MiB of HBM per device.

v0:
```python
import math
import jax
import jax.numpy as jnp
from jax import lax
from jax.sharding import PartitionSpec as P

CAP = 4


def body(feats_t, adj_index, adj_weight, weight, cotangent_t):
    feat_rows, node_cols = feats_t.shape
    blocks_n = adj_weight.shape[0]
    slots_n = adj_weight.shape[1]
    tile_n = adj_weight.shape[2]
    row_devs = lax.axis_size("rows")
    row_pos = lax.axis_index("rows")
    col_pos = lax.axis_index("cols")
    unit_rows = cotangent_t.shape[0]
    own_index = lax.dynamic_slice_in_dim(adj_index, row_pos * blocks_n, blocks_n, 0)
    own_flat = own_index.reshape(-1)
    local_tiles = feats_t.reshape(feat_rows, blocks_n, tile_n).transpose(1, 0, 2)
    device_ids = jnp.arange(row_devs, dtype=jnp.int32)
    slot_ids = jnp.arange(CAP, dtype=jnp.int32)
    mine = row_pos * blocks_n + jnp.arange(blocks_n, dtype=jnp.int32)
    peers_index = adj_index.reshape(row_devs, blocks_n * slots_n)
    wanted = (
        jnp.any(peers_index[:, :, None] == mine[None, None, :], axis=1)
        & (device_ids != row_pos)[:, None]
    )
    ordinal = jnp.cumsum(wanted.astype(jnp.int32), axis=1) - 1
    selector = wanted[:, None, :] & (ordinal[:, None, :] == slot_ids[None, :, None])
    source = own_flat // blocks_n
    block_pos = own_flat % blocks_n
    needed = jnp.any(
        own_flat[:, None] == jnp.arange(row_devs * blocks_n, dtype=jnp.int32)[None, :], axis=0
    )
    needed = needed.reshape(row_devs, blocks_n) & (device_ids != row_pos)[:, None]
    need_order = jnp.cumsum(needed.astype(jnp.int32), axis=1) - 1
    slot_of = source * CAP + need_order.reshape(-1)[own_flat]
    remote = source != row_pos
    outgoing = jnp.einsum(
        "pcb,bfj->pcfj",
        selector.astype(jnp.bfloat16),
        local_tiles,
        preferred_element_type=jnp.float32,
    ).astype(jnp.bfloat16)
    incoming = lax.all_to_all(outgoing, "rows", split_axis=0, concat_axis=0, tiled=True)
    received = incoming.reshape(row_devs * CAP, feat_rows, tile_n)[slot_of]
    own_part = local_tiles[block_pos]
    picked = jnp.where(remote[:, None, None], received, own_part).reshape(
        blocks_n, slots_n, feat_rows, tile_n
    )
    aggregate = jnp.einsum("bkfj,bkij->fbi", picked, adj_weight, preferred_element_type=jnp.float32)
    aggregated = aggregate.reshape(feat_rows, node_cols).astype(jnp.bfloat16)
    w_slab = lax.dynamic_slice_in_dim(weight, col_pos * unit_rows, unit_rows, 1)
    pre_act = lax.dot_general(
        w_slab,
        lax.all_gather(aggregated, "cols", axis=0, tiled=True),
        (((0,), (0,)), ((), ())),
        preferred_element_type=jnp.float32,
    )
    output_t = jax.nn.silu(pre_act).astype(jnp.bfloat16)
    sigm = jax.nn.sigmoid(pre_act)
    pre_grad = (cotangent_t.astype(jnp.float32) * sigm * (1.0 + pre_act * (1.0 - sigm))).astype(
        jnp.bfloat16
    )
    w_mine = lax.dynamic_slice_in_dim(weight, col_pos * feat_rows, feat_rows, 0)
    portion = lax.all_gather(pre_grad, "cols", axis=0, tiled=True)
    grad_acc = jnp.dot(w_mine, portion, preferred_element_type=jnp.float32)
    block_grad = lax.dot_general(
        aggregated, portion, (((1,), (1,)), ((), ())), preferred_element_type=jnp.float32
    )
    grad_scale = 1.0 / math.sqrt(node_cols * row_devs)
    weight_grad = lax.psum(block_grad, "rows") * grad_scale
    agg_grad = grad_acc.astype(jnp.bfloat16)
    contrib = jnp.einsum(
        "fbi,bkij->bkfj",
        agg_grad.reshape(feat_rows, blocks_n, tile_n),
        adj_weight,
        preferred_element_type=jnp.float32,
    )
    contrib_flat = contrib.reshape(blocks_n * slots_n, feat_rows * tile_n)
    slot_total = row_devs * CAP
    send_target = jnp.where(remote, slot_of, slot_total)
    sending = jax.ops.segment_sum(contrib_flat, send_target, num_segments=slot_total + 1)[
        :slot_total
    ]
    sending = sending.reshape(row_devs, CAP, feat_rows, tile_n)
    arrived = lax.all_to_all(
        sending.astype(jnp.bfloat16), "rows", split_axis=0, concat_axis=0, tiled=True
    ).astype(sending.dtype)
    arrived_flat = arrived.reshape(slot_total, feat_rows * tile_n)
    block_ids = jnp.arange(blocks_n, dtype=jnp.int32)
    slot_block = jnp.sum(selector.astype(jnp.int32) * block_ids[None, None, :], axis=2)
    slot_used = jnp.any(selector, axis=2)
    peer_target = jnp.where(slot_used, slot_block, blocks_n).reshape(-1)
    from_peers = jax.ops.segment_sum(arrived_flat, peer_target, num_segments=blocks_n + 1)[
        :blocks_n
    ]
    self_target = jnp.where(remote, blocks_n, block_pos)
    from_self = jax.ops.segment_sum(contrib_flat, self_target, num_segments=blocks_n + 1)[:blocks_n]
    summed = (from_peers + from_self).reshape(blocks_n, feat_rows, tile_n)
    feat_grad = summed.transpose(1, 0, 2).reshape(feat_rows, node_cols)
    return (output_t, weight_grad, feat_grad)


def solution(mesh):
    return jax.shard_map(
        body,
        mesh=mesh,
        in_specs=(P("cols", "rows"), P(), P("rows", None, None, None), P(), P("cols", "rows")),
        out_specs=(P("cols", "rows"), P("cols", None), P("cols", "rows")),
        check_vma=False,
    )
```

profile of v0, /device:TPU:0, one launch (start us, length us, event | category | flops | bytes accessed | tf_op | source)
XLA Modules:
  0.0 143.8 jit_solution(9876244328487271256)
XLA Ops:
  7.2 0.8 copy.41
  8.0 0.8 fusion.39
  9.8 0.9 copy.60
  10.9 0.7 copy.44
  11.7 7.3 %all-to-all-start = ((bf16[8,4,32,128]{3,2,1,0:T(8,128)(2,1)}), bf16[8,4,32,128]{3,2,1,0:T(8,128)(2,1)S(1)}, u32[]{:S(2)}, u32[]{:S(2)}) async-start(bf16[8,4,32,128]{3,2,1,0:T(8,128)(2,1)} %copy.44), calls=%async_computation | async-start | bytes 524288 | tf_op jit(solution)/shard_map/all_to_all | solution.py:47
  19.4 1.9 %gather_fusion = s32[256]{0:T(256)S(1)} fusion(s32[128]{0:T(128)S(1)} %sub.23, s32[1024]{0:T(1024)S(1)} %pad_clamp_fusion.2), kind=kCustom, calls=%fused_computation | custom fusion | bytes 3072 | tf_op jit(solution)/shard_map/gather | solution.py:39
  21.4 0.9 bitcast_bitcast_fusion
  22.3 1.0 gather_fusion.2
  23.4 4.6 %all-to-all-done = bf16[8,4,32,128]{3,2,1,0:T(8,128)(2,1)S(1)} async-done(((bf16[8,4,32,128]{3,2,1,0:T(8,128)(2,1)}), bf16[8,4,32,128]{3,2,1,0:T(8,128)(2,1)S(1)}, u32[]{:S(2)}, u32[]{:S(2)}) %all-to-all-start) | async-done | bytes 262176 | tf_op jit(solution)/shard_map/all_to_all | solution.py:47
  27.9 2.2 %gather_fusion.1 = bf16[256,32,128]{2,1,0:T(8,128)(2,1)} fusion(bf16[32,32,128]{2,1,0:T(8,128)(2,1)S(1)} %bitcast.83, s32[1024]{0:T(1024)S(1)} %pad_clamp_fusion.1), kind=kCustom, calls=%fused_computation.1 | custom fusion | bytes 4195328 | tf_op jit(solution)/shard_map/gather | solution.py:48
  30.1 6.9 %fusion.16 = bf16[16,4,8,128]{3,2,1,0:T(8,128)(2,1)S(1)} fusion(bf16[16,16,128,128]{3,2,1,0:T(8,128)(2,1)} %param.7, bf16[16,16,32,128]{3,2,1,0:T(8,128)(2,1)} %bitcast.85, bf16[16,16,32,128]{3,2,1,0:T(8,128)(2,1)S(1)} %bitcast.84, pred[16,16]{1,0:T(8,128)(4,1)S(1)} %copy.40), kind=kOutput, calls=%fused_computation.20 | convolution fusion | flops 269549568 | bytes 12714240 | tf_op jit(solution)/shard_map/bkfj,bkij->fbi/dot_general | solution.py:53
  37.1 7.3 %all_gather.6 = bf16[128,2048]{1,0:T(8,128)(2,1)S(1)} all-gather(bf16[32,2048]{1,0:T(8,128)(2,1)S(1)} %bitcast.90), channel_id=1, replica_groups=mesh['rows'=8,'cols'=4] {'cols'}, dimensions={0}, use_global_device_ids=true | all-gather | bytes 655360 | tf_op jit(solution)/shard_map/all_gather | solution.py:58
  44.4 1.3 multiply_convert_fusion
  46.2 14.7 %all-gather.2.cloned.1.call-done = bf16[256,2048]{1,0:T(8,128)(2,1)} async-done(((bf16[64,2048]{1,0:T(8,128)(2,1)}), bf16[256,2048]{1,0:T(8,128)(2,1)}) %all-gather.2.cloned.1.call-update) | async-done | bytes 1048592 | tf_op jit(solution)/shard_map/all_gather | solution.py:68
  60.9 1.5 %fusion.15 = bf16[4,8,16,128]{3,1,2,0:T(8,128)(2,1)S(1)} fusion(bf16[256,2048]{1,0:T(8,128)(2,1)} %all-gather.2.cloned.1.call-done, bf16[128,256]{1,0:T(8,128)(2,1)S(1)} %copy-done, s32[]{:T(128)S(6)} %select_n.136), kind=kOutput, calls=%fused_computation.19 | convolution fusion | flops 33619968 | bytes 1196036 | tf_op jit(solution)/shard_map/dot_general | solution.py:69
  62.5 6.5 %fusion.28 = f32[16,32,16,128]{3,1,2,0:T(8,128)} fusion(bf16[16,16,128,128]{3,2,1,0:T(8,128)(2,1)} %param.7, bf16[32,16,128,1]{2,1,0,3:T(8,128)(2,1)S(1)} %bitcast.88), kind=kOutput, calls=%fused_computation.38 | convolution fusion | flops 268435456 | bytes 12713984 | tf_op jit(solution)/shard_map/fbi,bkij->bkfj/dot_general | solution.py:76
  69.0 10.2 %scatter_custom_fusion.2 = f32[17,4096]{1,0:T(8,128)S(1)} fusion(s32[256]{0:T(256)S(1)} %bitcast.99, f32[32,8,32,128]{3,2,1,0:T(8,128)} %bitcast.81, f32[]{:T(128)} %constant.69.clone.1), kind=kCustom, calls=%fused_computation.6 | custom fusion | flops 1048576 | bytes 4472836 | tf_op jit(solution)/shard_map/scatter-add | solution.py:101
  79.3 10.2 %scatter_custom_fusion = f32[33,4096]{1,0:T(8,128)S(1)} fusion(s32[256]{0:T(256)S(1)} %bitcast.98, f32[32,8,32,128]{3,2,1,0:T(8,128)} %bitcast.82, f32[]{:T(128)} %constant.69.clone.1), kind=kCustom, calls=%fused_computation.8 | custom fusion | flops 1048576 | bytes 4734980 | tf_op jit(solution)/shard_map/scatter-add | solution.py:85
  89.5 0.7 copy.63
  90.3 5.5 %all-to-all-start.1 = ((bf16[8,4,32,128]{3,2,1,0:T(8,128)(2,1)}), bf16[8,4,32,128]{3,2,1,0:T(8,128)(2,1)S(1)}, u32[]{:S(2)}, u32[]{:S(2)}) async-start(bf16[8,4,32,128]{3,2,1,0:T(8,128)(2,1)} %bitcast.37), calls=%async_computation.1 | async-start | bytes 524288 | tf_op jit(solution)/shard_map/all_to_all | solution.py:89
  96.2 37.6 %psum.7 = f32[32,256]{1,0:T(8,128)S(1)} all-reduce(f32[32,256]{1,0:T(8,128)S(1)} %fusion.45), channel_id=1, replica_groups=mesh['rows'=8,'cols'=4] {'rows'}, use_global_device_ids=true, to_apply=%region_4.5 | all-reduce | flops 8192 | bytes 65536 | tf_op jit(solution)/shard_map/psum | solution.py:74
  133.8 0.6 broadcast_multiply_fusion
  134.4 1.7 %scatter_custom_fusion.1 = f32[17,4096]{1,0:T(8,128)S(1)} fusion(s32[32]{0:T(128)S(1)} %reshape.376, f32[4,8,32,128]{3,2,1,0:T(8,128)S(1)} %bitcast_convert_fusion, f32[]{:T(128)} %constant.69.clone.1), kind=kCustom, calls=%fused_computation.21 | custom fusion | flops 131072 | bytes 802820 | tf_op jit(solution)/shard_map/scatter-add | solution.py:97
  136.2 0.7 copy.84
  (44 shorter events, 2.8 us)
Async XLA Ops:
  7.2 37.3 %copy-start = (bf16[128,256]{1,0:T(8,128)(2,1)S(1)}, bf16[128,256]{1,0:T(8,128)(2,1)}, u32[]{:S(2)}) copy-start(bf16[128,256]{1,0:T(8,128)(2,1)} %param.8) | copy-start | bytes 196612
  11.7 16.2 %all-to-all-start = ((bf16[8,4,32,128]{3,2,1,0:T(8,128)(2,1)}), bf16[8,4,32,128]{3,2,1,0:T(8,128)(2,1)S(1)}, u32[]{:S(2)}, u32[]{:S(2)}) async-start(bf16[8,4,32,128]{3,2,1,0:T(8,128)(2,1)} %copy.44), calls=%async_computation | async-start | bytes 524288 | tf_op jit(solution)/shard_map/all_to_all | solution.py:47
  19.0 41.9 %all-gather.2.cloned.1.call-start = ((), (), s32[]{:S(2)}) async-start(), calls=%async_computation.2 | async-start | bytes 1310720 | tf_op jit(solution)/shard_map/all_gather | solution.py:68
  30.1 14.3 %copy-start.2 = (bf16[64,2048]{1,0:T(8,128)(2,1)S(1)}, bf16[64,2048]{1,0:T(8,128)(2,1)}, u32[]{:S(2)}) copy-start(bf16[64,2048]{1,0:T(8,128)(2,1)} %param.9) | copy-start | bytes 786436
  79.3 16.5 %copy-start.1 = (bf16[256,2048]{1,0:T(8,128)(2,1)S(1)}, bf16[256,2048]{1,0:T(8,128)(2,1)}, u32[]{:S(2)}) copy-start(bf16[256,2048]{1,0:T(8,128)(2,1)} %all-gather.2.cloned.1.call-done) | copy-start | bytes 3145732
  90.3 44.1 %all-to-all-start.1 = ((bf16[8,4,32,128]{3,2,1,0:T(8,128)(2,1)}), bf16[8,4,32,128]{3,2,1,0:T(8,128)(2,1)S(1)}, u32[]{:S(2)}, u32[]{:S(2)}) async-start(bf16[8,4,32,128]{3,2,1,0:T(8,128)(2,1)} %bitcast.37), calls=%async_computation.1 | async-start | bytes 524288 | tf_op jit(solution)/shard_map/all_to_all | solution.py:89
Sparse Core Ops, SparseCore 0:
  45.9 15.0 all-gather.1
where the time goes:
time: 144 us
  blocking collectives  44.9 us (31%)
  other arithmetic  24.7 us (17%)
  waiting for transfers between devices  19.3 us (13%)
  matrix products  16.9 us (12%)
  between operations  14.2 us (10%)
  starting transfers between devices  12.9 us (9%)
  local copies, waits for them, and re-layouts  10.8 us (8%)
    psum x1, blocking collectives, body(): weight_grad = lax.psum(block_grad, 'rows') * grad_scale  37.6 us
    all_gather x1, waiting for transfers between devices, body(): portion = lax.all_gather(pre_grad, 'cols', axis=0, tiled=True)  14.7 us
    scatter-add x1, other arithmetic, body(): jax.ops.segment_sum(contrib_flat, self_target, num_segments=blocks_n + 1)  10.2 us
    scatter-add x1, other arithmetic, body(): jax.ops.segment_sum(contrib_flat, send_target, num_segments=slot_total + 1)  10.2 us
    all_gather x1, blocking collectives, body(): lax.all_gather(aggregated, 'cols', axis=0, tiled=True)  7.35 us
    all_to_all x1, starting transfers between devices, body(): lax.all_to_all(outgoing, 'rows', split_axis=0, concat_axis=0, tiled=True)  7.31 us
    dot_general x1, matrix products, body(): jnp.einsum('bkfj,bkij->fbi', picked, adj_weight, preferred_element_type=j...  6.91 us
    dot_general x1, matrix products, body(): jnp.einsum('fbi,bkij->bkfj', agg_grad.reshape(feat_rows, blocks_n, tile_n...  6.54 us
  transfers between devices with their start and end apart: 3, of which 2 were waited for; matrix products, arithmetic and copies ran while one was open for 4% of the time, Pallas kernels for 0%

commit v1 on v0

--- a/solution.py
+++ b/solution.py
@@ -71,7 +71,7 @@
         aggregated, portion, (((1,), (1,)), ((), ())), preferred_element_type=jnp.float32
     )
     grad_scale = 1.0 / math.sqrt(node_cols * row_devs)
-    weight_grad = lax.psum(block_grad, "rows") * grad_scale
+    weight_grad = jnp.sum(lax.all_gather(block_grad, "rows"), axis=0) * grad_scale
     agg_grad = grad_acc.astype(jnp.bfloat16)
     contrib = jnp.einsum(
         "fbi,bkij->bkfj",

time: 144 us -> 140 us (0.972)
  blocking collectives: 44.9 us -> 40.6 us
    psum x1 -> x0, blocking collectives: 37.6 us -> none  [body(): weight_grad = lax.psum(block_grad, 'rows') * grad_scale]
    all_gather x0 -> x1, blocking collectives: none -> 33.3 us  [body(): lax.all_gather(block_grad, 'rows')]
  transfers between devices with their start and end apart: 3 -> 3, of which waited for: 2 -> 2; matrix products, arithmetic and copies ran while one was open for 4% -> 11% of each run, Pallas kernels for 0% -> 0%
where the time goes in v1:
time: 140 us; the launch traced here: 139 us
  blocking collectives  40.6 us (29%)
  other arithmetic  24.5 us (18%)
  waiting for transfers between devices  19.3 us (14%)
  matrix products  16.9 us (12%)
  between operations  14.2 us (10%)
  starting transfers between devices  12.9 us (9%)
  local copies, waits for them, and re-layouts  10.8 us (8%)
    all_gather x1, blocking collectives, body(): lax.all_gather(block_grad, 'rows')  33.3 us
    all_gather x1, waiting for transfers between devices, body(): portion = lax.all_gather(pre_grad, 'cols', axis=0, tiled=True)  14.7 us
    scatter-add x1, other arithmetic, body(): jax.ops.segment_sum(contrib_flat, send_target, num_segments=slot_total + 1)  10.2 us
    scatter-add x1, other arithmetic, body(): jax.ops.segment_sum(contrib_flat, self_target, num_segments=blocks_n + 1)  10 us
    all_gather x1, blocking collectives, body(): lax.all_gather(aggregated, 'cols', axis=0, tiled=True)  7.35 us
    all_to_all x1, starting transfers between devices, body(): lax.all_to_all(outgoing, 'rows', split_axis=0, concat_axis=0, tiled=True)  7.31 us
    dot_general x1, matrix products, body(): jnp.einsum('bkfj,bkij->fbi', picked, adj_weight, preferred_element_type=j...  6.91 us
    dot_general x1, matrix products, body(): jnp.einsum('fbi,bkij->bkfj', agg_grad.reshape(feat_rows, blocks_n, tile_n...  6.54 us
  transfers between devices with their start and end apart: 3, of which 2 were waited for; matrix products, arithmetic and copies ran while one was open for 11% of the time, Pallas kernels for 0%

profile of v1, /device:TPU:0, one launch (start us, length us, event | category | flops | bytes accessed | tf_op | source)
XLA Modules:
  0.0 139.3 jit_solution(4189667286631378425)
XLA Ops:
  7.2 0.8 copy.41
  8.0 0.8 fusion.39
  9.8 0.9 copy.60
  10.9 0.7 copy.44
  11.7 7.3 %all-to-all-start = ((bf16[8,4,32,128]{3,2,1,0:T(8,128)(2,1)}), bf16[8,4,32,128]{3,2,1,0:T(8,128)(2,1)S(1)}, u32[]{:S(2)}, u32[]{:S(2)}) async-start(bf16[8,4,32,128]{3,2,1,0:T(8,128)(2,1)} %copy.44), calls=%async_computation | async-start | bytes 524288 | tf_op jit(solution)/shard_map/all_to_all | solution.py:47
  19.4 1.9 %gather_fusion = s32[256]{0:T(256)S(1)} fusion(s32[128]{0:T(128)S(1)} %sub.23, s32[1024]{0:T(1024)S(1)} %pad_clamp_fusion.2), kind=kCustom, calls=%fused_computation | custom fusion | bytes 3072 | tf_op jit(solution)/shard_map/gather | solution.py:39
  21.4 0.9 bitcast_bitcast_fusion
  22.3 1.0 gather_fusion.2
  23.4 4.6 %all-to-all-done = bf16[8,4,32,128]{3,2,1,0:T(8,128)(2,1)S(1)} async-done(((bf16[8,4,32,128]{3,2,1,0:T(8,128)(2,1)}), bf16[8,4,32,128]{3,2,1,0:T(8,128)(2,1)S(1)}, u32[]{:S(2)}, u32[]{:S(2)}) %all-to-all-start) | async-done | bytes 262176 | tf_op jit(solution)/shard_map/all_to_all | solution.py:47
  27.9 2.2 %gather_fusion.1 = bf16[256,32,128]{2,1,0:T(8,128)(2,1)} fusion(bf16[32,32,128]{2,1,0:T(8,128)(2,1)S(1)} %bitcast.84, s32[1024]{0:T(1024)S(1)} %pad_clamp_fusion.1), kind=kCustom, calls=%fused_computation.1 | custom fusion | bytes 4195328 | tf_op jit(solution)/shard_map/gather | solution.py:48
  30.1 6.9 %fusion.16 = bf16[16,4,8,128]{3,2,1,0:T(8,128)(2,1)S(1)} fusion(bf16[16,16,128,128]{3,2,1,0:T(8,128)(2,1)} %param.7, bf16[16,16,32,128]{3,2,1,0:T(8,128)(2,1)} %bitcast.86, bf16[16,16,32,128]{3,2,1,0:T(8,128)(2,1)S(1)} %bitcast.85, pred[16,16]{1,0:T(8,128)(4,1)S(1)} %copy.40), kind=kOutput, calls=%fused_computation.20 | convolution fusion | flops 269549568 | bytes 12714240 | tf_op jit(solution)/shard_map/bkfj,bkij->fbi/dot_general | solution.py:53
  37.1 7.3 %all_gather.12 = bf16[128,2048]{1,0:T(8,128)(2,1)S(1)} all-gather(bf16[32,2048]{1,0:T(8,128)(2,1)S(1)} %bitcast.92), channel_id=1, replica_groups=mesh['rows'=8,'cols'=4] {'cols'}, dimensions={0}, use_global_device_ids=true | all-gather | bytes 655360 | tf_op jit(solution)/shard_map/all_gather | solution.py:58
  44.4 1.3 multiply_convert_fusion
  46.2 14.7 %all-gather.3.cloned.1.call-done = bf16[256,2048]{1,0:T(8,128)(2,1)} async-done(((bf16[64,2048]{1,0:T(8,128)(2,1)}), bf16[256,2048]{1,0:T(8,128)(2,1)}) %all-gather.3.cloned.1.call-update) | async-done | bytes 1048592 | tf_op jit(solution)/shard_map/all_gather | solution.py:68
  60.9 1.5 %fusion.15 = bf16[4,8,16,128]{3,1,2,0:T(8,128)(2,1)S(1)} fusion(bf16[256,2048]{1,0:T(8,128)(2,1)} %all-gather.3.cloned.1.call-done, bf16[128,256]{1,0:T(8,128)(2,1)S(1)} %copy-done, s32[]{:T(128)S(6)} %select_n.136), kind=kOutput, calls=%fused_computation.19 | convolution fusion | flops 33619968 | bytes 1196036 | tf_op jit(solution)/shard_map/dot_general | solution.py:69
  62.5 6.5 %fusion.28 = f32[16,32,16,128]{3,1,2,0:T(8,128)} fusion(bf16[16,16,128,128]{3,2,1,0:T(8,128)(2,1)} %param.7, bf16[32,16,128,1]{2,1,0,3:T(8,128)(2,1)S(1)} %bitcast.90), kind=kOutput, calls=%fused_computation.38 | convolution fusion | flops 268435456 | bytes 12713984 | tf_op jit(solution)/shard_map/fbi,bkij->bkfj/dot_general | solution.py:76
  69.0 10.2 %scatter_custom_fusion = f32[33,4096]{1,0:T(8,128)S(1)} fusion(s32[256]{0:T(256)S(1)} %bitcast.101, f32[32,8,32,128]{3,2,1,0:T(8,128)} %bitcast.82, f32[]{:T(128)} %constant.69.clone.1), kind=kCustom, calls=%fused_computation.8 | custom fusion | flops 1048576 | bytes 4734980 | tf_op jit(solution)/shard_map/scatter-add | solution.py:85
  79.2 0.7 copy.63
  80.0 5.5 %all-to-all-start.1 = ((bf16[8,4,32,128]{3,2,1,0:T(8,128)(2,1)}), bf16[8,4,32,128]{3,2,1,0:T(8,128)(2,1)S(1)}, u32[]{:S(2)}, u32[]{:S(2)}) async-start(bf16[8,4,32,128]{3,2,1,0:T(8,128)(2,1)} %bitcast.38), calls=%async_computation.1 | async-start | bytes 524288 | tf_op jit(solution)/shard_map/all_to_all | solution.py:89
  85.9 33.3 %all-gather = f32[256,256]{1,0:T(8,128)S(1)} all-gather(f32[32,256]{1,0:T(8,128)S(1)} %fusion.45), channel_id=2, replica_groups=mesh['rows'=8,'cols'=4] {'rows'}, dimensions={0}, use_global_device_ids=true | all-gather | bytes 294912 | tf_op jit(solution)/shard_map/all_gather | solution.py:74
  119.2 10.0 %scatter_custom_fusion.2 = f32[17,4096]{1,0:T(8,128)S(1)} fusion(s32[256]{0:T(256)S(1)} %bitcast.100, f32[32,8,32,128]{3,2,1,0:T(8,128)} %bitcast.83, f32[]{:T(128)} %constant.69.clone.1), kind=kCustom, calls=%fused_computation.6 | custom fusion | flops 1048576 | bytes 4472836 | tf_op jit(solution)/shard_map/scatter-add | solution.py:101
  129.2 0.6 broadcast_multiply_fusion
  129.9 1.7 %scatter_custom_fusion.1 = f32[17,4096]{1,0:T(8,128)S(1)} fusion(s32[32]{0:T(128)S(1)} %reshape.376, f32[4,8,32,128]{3,2,1,0:T(8,128)S(1)} %bitcast_convert_fusion, f32[]{:T(128)} %constant.69.clone.1), kind=kCustom, calls=%fused_computation.21 | custom fusion | flops 131072 | bytes 802820 | tf_op jit(solution)/shard_map/scatter-add | solution.py:97
  131.7 0.7 copy.84
  (45 shorter events, 2.9 us)
Async XLA Ops:
  7.2 37.3 %copy-start = (bf16[128,256]{1,0:T(8,128)(2,1)S(1)}, bf16[128,256]{1,0:T(8,128)(2,1)}, u32[]{:S(2)}) copy-start(bf16[128,256]{1,0:T(8,128)(2,1)} %param.8) | copy-start | bytes 196612
  11.7 16.2 %all-to-all-start = ((bf16[8,4,32,128]{3,2,1,0:T(8,128)(2,1)}), bf16[8,4,32,128]{3,2,1,0:T(8,128)(2,1)S(1)}, u32[]{:S(2)}, u32[]{:S(2)}) async-start(bf16[8,4,32,128]{3,2,1,0:T(8,128)(2,1)} %copy.44), calls=%async_computation | async-start | bytes 524288 | tf_op jit(solution)/shard_map/all_to_all | solution.py:47
  19.0 41.9 %all-gather.3.cloned.1.call-start = ((), (), s32[]{:S(2)}) async-start(), calls=%async_computation.2 | async-start | bytes 1310720 | tf_op jit(solution)/shard_map/all_gather | solution.py:68
  30.1 14.3 %copy-start.2 = (bf16[64,2048]{1,0:T(8,128)(2,1)S(1)}, bf16[64,2048]{1,0:T(8,128)(2,1)}, u32[]{:S(2)}) copy-start(bf16[64,2048]{1,0:T(8,128)(2,1)} %param.9) | copy-start | bytes 786436
  69.0 16.5 %copy-start.1 = (bf16[256,2048]{1,0:T(8,128)(2,1)S(1)}, bf16[256,2048]{1,0:T(8,128)(2,1)}, u32[]{:S(2)}) copy-start(bf16[256,2048]{1,0:T(8,128)(2,1)} %all-gather.3.cloned.1.call-done) | copy-start | bytes 3145732
  80.0 49.9 %all-to-all-start.1 = ((bf16[8,4,32,128]{3,2,1,0:T(8,128)(2,1)}), bf16[8,4,32,128]{3,2,1,0:T(8,128)(2,1)S(1)}, u32[]{:S(2)}, u32[]{:S(2)}) async-start(bf16[8,4,32,128]{3,2,1,0:T(8,128)(2,1)} %bitcast.38), calls=%async_computation.1 | async-start | bytes 524288 | tf_op jit(solution)/shard_map/all_to_all | solution.py:89
Sparse Core Ops, SparseCore 0:
  45.9 15.0 all-gather.2
